TPU v7x, 128 devices: a whole 4x4x4 slice. The times are simulated.
128 devices in a mesh: pipe: 16 (over y_lo, z, core), seq: 8 (over x, y_hi).
Axes of the slice: x: 4, y: 4 (y_hi: 2, y_lo: 2; y = y_hi * 2 + y_lo), z: 4, core: 2. Of those that a mesh axis runs over, the one named last changes fastest.
Arguments:
- x_fwd: float32 [16, 1024, 2048], P('pipe', 'seq'), may hold values from -12 to 12
- x_bwd: float32 [16, 1024, 2048], P('pipe', 'seq'), may hold values from -12 to 12
- grad_in: float32 [16, 1024, 2048], P('pipe', 'seq'), may hold values from -6 to 6
- gain: float32 [16, 2048], P('pipe'), may hold values from 0.25 to 1.75
- w_query: bfloat16 [16, 2048, 2048], P('pipe', None, 'seq'), may hold values from -2 to 2
- w_key: bfloat16 [16, 2048, 2048], P('pipe', None, 'seq'), may hold values from -2 to 2
- w_value: bfloat16 [16, 2048, 2048], P('pipe', None, 'seq'), may hold values from -0.125 to 0.125
- w_out: bfloat16 [16, 2048, 2048], P('pipe', None, 'seq'), may hold values from -0.125 to 0.125
Outputs:
- act_next: float32 [16, 1024, 2048], P('pipe', 'seq')
- grad_prev: float32 [16, 1024, 2048], P('pipe', 'seq')
All inputs are finite; a program needn't handle non-finite values.
Results may differ from a plain program's by a relative error of at most 0.012.
The roundings to bfloat16 on the way count: a program that leaves them out, or rounds other values in their place, can miss the bound.
Values may be sent and summed in bfloat16 or wider, within the bound.
A program may use at most 192 MiB of HBM per device.

v0:
```python
import jax
import jax.numpy as jnp
from jax import lax
from jax.sharding import PartitionSpec as P

HD = 128


def passed_along(value, axis, steps):
    count = lax.axis_size(axis)
    pairs = [(source, (source + steps) % count) for source in range(count)]
    return lax.ppermute(value, axis, pairs)


def rope_tables(positions):
    half_dim = HD // 2
    inverse = 10000.0 ** (-(jnp.arange(half_dim).astype(jnp.float32) * 2.0 / HD))
    angles = positions.astype(jnp.float32)[:, None] * inverse[None, :]
    return (jnp.cos(angles)[:, None, :], jnp.sin(angles)[:, None, :])


def rotate(values, cosine, sine_table):
    shaped = values.reshape(values.shape[0], -1, HD)
    first_half = shaped[..., : HD // 2]
    second_half = shaped[..., HD // 2 :]
    output = jnp.concatenate(
        [
            first_half * cosine - second_half * sine_table,
            second_half * cosine + first_half * sine_table,
        ],
        -1,
    )
    return output.reshape(values.shape)


def rotate_back(values, cosine, sine_table):
    shaped = values.reshape(values.shape[0], -1, HD)
    first_half = shaped[..., : HD // 2]
    second_half = shaped[..., HD // 2 :]
    output = jnp.concatenate(
        [
            first_half * cosine + second_half * sine_table,
            second_half * cosine - first_half * sine_table,
        ],
        -1,
    )
    return output.reshape(values.shape)


def normalize(inputs, gain_row):
    inv_rms = lax.rsqrt(jnp.mean(inputs * inputs, -1, keepdims=True) + 1e-05)
    return ((inputs * inv_rms * gain_row).astype(jnp.bfloat16), inv_rms)


def times_t(left, right):
    return lax.dot_general(
        left, right, (((1,), (1,)), ((), ())), preferred_element_type=jnp.float32
    )


def split_heads(values):
    return values.reshape(values.shape[0], -1, HD)


def attend(query, key_rows, value_rows):
    length = query.shape[0]
    score_scale = HD ** (-0.5)
    key_heads = split_heads(key_rows)
    value_heads = split_heads(value_rows)
    query_blocks = split_heads(query).reshape(length // length, length, -1, HD)

    def one_block(query_block):
        scores = (
            jnp.einsum("qhd,khd->hqk", query_block, key_heads, preferred_element_type=jnp.float32)
            * score_scale
        )
        probs = jax.nn.softmax(scores, axis=-1)
        output = jnp.einsum(
            "hqk,khd->qhd",
            probs.astype(jnp.bfloat16),
            value_heads,
            preferred_element_type=jnp.float32,
        )
        return output.astype(jnp.bfloat16)

    return lax.map(one_block, query_blocks).reshape(length, -1)


def attend_back(query, key_rows, value_rows, grad_out, cosine, sine_table):
    length = query.shape[0]
    score_scale = HD ** (-0.5)
    key_heads = split_heads(key_rows)
    value_heads = split_heads(value_rows)
    query_blocks = split_heads(query).reshape(length // length, length, -1, HD)
    grad_blocks = split_heads(grad_out).reshape(length // length, length, -1, HD)

    def step(totals, operands):
        query_block, grad_block = operands
        scores = (
            jnp.einsum("qhd,khd->hqk", query_block, key_heads, preferred_element_type=jnp.float32)
            * score_scale
        )
        probs = jax.nn.softmax(scores, axis=-1)
        value_grad = jnp.einsum(
            "hqk,qhd->khd",
            probs.astype(jnp.bfloat16),
            grad_block,
            preferred_element_type=jnp.float32,
        )
        prob_grad = jnp.einsum(
            "qhd,khd->hqk", grad_block, value_heads, preferred_element_type=jnp.float32
        )
        row_delta = jnp.sum(probs * prob_grad, -1, keepdims=True)
        score_grad = (probs * (prob_grad - row_delta) * score_scale).astype(jnp.bfloat16)
        query_grad = jnp.einsum(
            "hqk,khd->qhd", score_grad, key_heads, preferred_element_type=jnp.float32
        )
        key_grad = jnp.einsum(
            "hqk,qhd->khd", score_grad, query_block, preferred_element_type=jnp.float32
        )
        return ((totals[0] + key_grad, totals[1] + value_grad), query_grad)

    zero_heads = jnp.zeros(key_heads.shape, jnp.float32)
    (key_total, value_total), query_grads = lax.scan(
        step, (zero_heads, zero_heads), (query_blocks, grad_blocks)
    )
    query_grad = rotate_back(query_grads.reshape(length, -1), cosine, sine_table).astype(
        jnp.bfloat16
    )
    key_grad = rotate_back(key_total.reshape(length, -1), cosine, sine_table).astype(jnp.bfloat16)
    return (query_grad, key_grad, value_total.reshape(length, -1).astype(jnp.bfloat16))


def to_tokens(values):
    return lax.all_to_all(values, "seq", split_axis=1, concat_axis=2, tiled=True)


def shards(x_fwd, x_bwd, grad_in, gain, w_query, w_key, w_value, w_out):
    act_in = x_fwd[0]
    saved_in = x_bwd[0]
    grad = grad_in[0]
    gain_row = gain[0]
    local_rows = act_in.shape[0]
    length = local_rows * lax.axis_size("seq")
    normed_fwd, inv_fwd = normalize(act_in, gain_row)
    normed_bwd, inv_bwd = normalize(saved_in, gain_row)
    grad_low = grad.astype(jnp.bfloat16)
    full_cos, full_sin = rope_tables(jnp.arange(length))
    all_query, all_key, all_value, all_out = (
        lax.all_gather(w_query[0], "seq", axis=1, tiled=True),
        lax.all_gather(w_key[0], "seq", axis=1, tiled=True),
        lax.all_gather(w_value[0], "seq", axis=1, tiled=True),
        lax.all_gather(w_out[0], "seq", axis=1, tiled=True),
    )
    local_cos, local_sin = rope_tables(lax.axis_index("seq") * local_rows + jnp.arange(local_rows))

    def project_local(normed):
        query = rotate(
            jnp.dot(normed, all_query, preferred_element_type=jnp.float32), local_cos, local_sin
        ).astype(jnp.bfloat16)
        key_rows = rotate(
            jnp.dot(normed, all_key, preferred_element_type=jnp.float32), local_cos, local_sin
        ).astype(jnp.bfloat16)
        value_rows = jnp.dot(normed, all_value, preferred_element_type=jnp.float32).astype(
            jnp.bfloat16
        )
        return [query, key_rows, value_rows]

    attn_grad = jnp.dot(grad_low, all_out, preferred_element_type=jnp.float32).astype(jnp.bfloat16)
    pieces = jnp.stack(project_local(normed_fwd) + project_local(normed_bwd) + [attn_grad])
    head_view = lax.all_to_all(pieces, "seq", split_axis=2, concat_axis=1, tiled=True)
    attn = attend(head_view[0], head_view[1], head_view[2])
    attn_tokens = to_tokens(attn[None])[0]
    branch = times_t(attn_tokens, all_out)
    query_grad, key_grad, value_grad = attend_back(
        head_view[3], head_view[4], head_view[5], head_view[6], full_cos, full_sin
    )
    grad_tokens = to_tokens(jnp.stack([query_grad, key_grad, value_grad]))
    d_normed = (
        times_t(grad_tokens[0], all_query)
        + times_t(grad_tokens[1], all_key)
        + times_t(grad_tokens[2], all_value)
    )
    act_out = act_in + branch
    gain_grad = d_normed * gain_row
    d_input = inv_bwd * gain_grad - saved_in * inv_bwd * inv_bwd * inv_bwd * jnp.mean(
        saved_in * gain_grad, -1, keepdims=True
    )
    sent_forward = passed_along(act_out.astype(jnp.bfloat16), "pipe", 1).astype(act_out.dtype)
    sent_backward = passed_along((grad + d_input).astype(jnp.bfloat16), "pipe", -1).astype(
        jnp.float32
    )
    return (sent_forward[None], sent_backward[None])


def solution(mesh):
    placed = (
        P("pipe", "seq", None),
        P("pipe", "seq", None),
        P("pipe", "seq", None),
        P("pipe", None),
        P("pipe", None, "seq"),
        P("pipe", None, "seq"),
        P("pipe", None, "seq"),
        P("pipe", None, "seq"),
    )
    return jax.shard_map(
        shards,
        mesh=mesh,
        in_specs=placed,
        out_specs=(P("pipe", "seq", None), P("pipe", "seq", None)),
        check_vma=False,
    )
```

profile of v0, /device:TPU:1, one launch (start us, length us, event | category | flops | bytes accessed | tf_op | source)
XLA Modules:
  0.0 765.0 jit_solution(12762140533666074192)
XLA Ops:
  13.0 118.5 %all-gather.11.cloned.1.call-done = bf16[1,2048,2048]{2,1,0:T(8,128)(2,1)} async-done(((bf16[1,2048,256]{2,1,0:T(8,128)(2,1)}), bf16[1,2048,2048]{2,1,0:T(8,128)(2,1)}) %all-gather.11.cloned.1.call-update) | async-done | bytes 8388624 | tf_op jit(solution)/shard_map/all_gather | solution.py:151
  131.5 12.4 %copy.67 = bf16[2048,2048]{1,0:T(8,128)(2,1)} copy(bf16[2048,2048]{0,1:T(8,128)(2,1)} %bitcast.212) | data formatting | bytes 16777216 | tf_op jit(solution)/shard_map/dot_general | solution.py:162
  143.8 108.1 %all-gather.9.cloned.1.call-done = bf16[1,2048,2048]{2,1,0:T(8,128)(2,1)} async-done(((bf16[1,2048,256]{2,1,0:T(8,128)(2,1)}), bf16[1,2048,2048]{2,1,0:T(8,128)(2,1)}) %all-gather.9.cloned.1.call-update) | async-done | bytes 8388624 | tf_op jit(solution)/shard_map/all_gather | solution.py:150
  251.9 12.4 %copy.66 = bf16[2048,2048]{1,0:T(8,128)(2,1)} copy(bf16[2048,2048]{0,1:T(8,128)(2,1)} %bitcast.213) | data formatting | bytes 16777216 | tf_op jit(solution)/shard_map/dot_general | solution.py:159
  264.3 6.5 fusion.112
  292.4 80.0 %all-gather.13.cloned.1.call-done = bf16[1,2048,2048]{2,1,0:T(8,128)(2,1)} async-done(((bf16[1,2048,256]{2,1,0:T(8,128)(2,1)}), bf16[1,2048,2048]{2,1,0:T(8,128)(2,1)}) %all-gather.13.cloned.1.call-update) | async-done | bytes 8388624 | tf_op jit(solution)/shard_map/all_gather | solution.py:152
  372.5 5.6 fusion.76
  382.4 110.4 %all-gather.15.cloned.1.call-done = bf16[1,2048,2048]{2,1,0:T(8,128)(2,1)} async-done(((bf16[1,2048,256]{2,1,0:T(8,128)(2,1)}), bf16[1,2048,2048]{2,1,0:T(8,128)(2,1)}) %all-gather.15.cloned.1.call-update) | async-done | bytes 8388624 | tf_op jit(solution)/shard_map/all_gather | solution.py:153
  492.8 5.4 fusion.64
  498.3 6.5 copy.72
  504.7 4.5 all-to-all-start
  511.1 56.6 %all-to-all-done = bf16[7,128,2048]{1,0,2:T(8,128)(2,1)} async-done(((bf16[7,128,2048]{1,0,2:T(8,128)(2,1)}), bf16[7,128,2048]{1,0,2:T(8,128)(2,1)}, u32[]{:S(2)}, u32[]{:S(2)}) %all-to-all-start) | async-done | bytes 3670048 | tf_op jit(solution)/shard_map/all_to_all | solution.py:171
  567.7 4.8 copy.105
  582.7 5.7 fusion.127
  588.4 7.2 fusion.124
  595.6 5.9 fusion.86
  601.5 14.8 %fusion.82 = f32[1024,2,128]{0,2,1:T(8,128)} fusion(bf16[1024,2,128]{0,2,1:T(8,128)(2,1)} %squeeze.55, f32[2,1024,1024]{1,2,0:T(8,128)} %fusion.127, f32[2,1024,1024]{1,2,0:T(8,128)} %get-tuple-element.78, f32[2,1024]{1,0:T(2,128)S(1)} %get-tuple-element.77), kind=kOutput, calls=%fused_computation.52 | convolution fusion | flops 551554048 | bytes 18358272 | tf_op jit(solution)/shard_map/while/body/eval_jaxpr/hqk,qhd->khd/dot_general | solution.py:118
  616.2 14.8 %fusion.79 = f32[1024,2,128]{0,2,1:T(8,128)} fusion(bf16[1024,2,128]{0,2,1:T(8,128)(2,1)} %reshape_squeeze.14, f32[2,1024,1024]{1,2,0:T(8,128)} %fusion.127, f32[2,1024,1024]{1,2,0:T(8,128)} %get-tuple-element.78, f32[2,1024]{1,0:T(2,128)S(1)} %get-tuple-element.77), kind=kOutput, calls=%fused_computation.51 | convolution fusion | flops 551554048 | bytes 18358272 | tf_op jit(solution)/shard_map/while/body/eval_jaxpr/hqk,khd->qhd/dot_general | solution.py:115
  637.3 7.2 fusion.123
  644.5 5.1 fusion.85
  649.6 3.6 copy.77
  653.7 5.6 reduce
  661.3 4.4 all-to-all-start.1
  672.8 3.6 copy.86
  681.8 6.0 pad_maximum_fusion
  687.7 6.6 all-to-all-start.2
  702.0 7.3 fusion.58
  709.2 4.0 collective-permute-start
  713.3 9.9 %all-to-all-done.2 = bf16[3,1024,256]{2,0,1:T(4,128)(2,1)} async-done(((bf16[3,1024,256]{2,0,1:T(4,128)(2,1)}), bf16[3,1024,256]{2,0,1:T(4,128)(2,1)}, u32[]{:S(2)}, u32[]{:S(2)}) %all-to-all-start.2) | async-done | bytes 1572896 | tf_op jit(solution)/shard_map/all_to_all | solution.py:135
  730.0 6.6 fusion.13
  736.6 6.5 fusion.37
  751.0 5.9 collective-permute-done.1
  (89 shorter events, 88.2 us)
Async XLA Ops:
  7.2 124.3 %all-gather.11.cloned.1.call-start = ((), (), s32[]{:S(2)}) async-start(), calls=%async_computation.4 | async-start | bytes 9437184 | tf_op jit(solution)/shard_map/all_gather | solution.py:151
  7.9 244.0 %all-gather.9.cloned.1.call-start = ((), (), s32[]{:S(2)}) async-start(), calls=%async_computation.3 | async-start | bytes 9437184 | tf_op jit(solution)/shard_map/all_gather | solution.py:150
  8.6 363.8 %all-gather.13.cloned.1.call-start = ((), (), s32[]{:S(2)}) async-start(), calls=%async_computation.5 | async-start | bytes 9437184 | tf_op jit(solution)/shard_map/all_gather | solution.py:152
  9.4 483.4 %all-gather.15.cloned.1.call-start = ((), (), s32[]{:S(2)}) async-start(), calls=%async_computation.6 | async-start | bytes 9437184 | tf_op jit(solution)/shard_map/all_gather | solution.py:153
  251.9 12.4 %copy-start.2 = (f32[1,128,2048]{2,1,0:T(8,128)S(1)}, f32[1,128,2048]{2,1,0:T(8,128)}, u32[]{:S(2)}) copy-start(f32[1,128,2048]{2,1,0:T(8,128)} %param.9) | copy-start | bytes 3145732
  251.9 12.4 %copy-start.7 = (f32[1,2048]{1,0:T(1,128)S(1)}, f32[1,2048]{1,0:T(1,128)}, u32[]{:S(2)}) copy-start(f32[1,2048]{1,0:T(1,128)} %param.11) | copy-start | bytes 24580
  264.3 6.5 copy-start.1
  264.3 6.6 copy-start.3
  264.3 9.1 %slice-start.2 = ((s8[8388608]{0:T(1024)(128)(4,1)}), s8[4194304]{0:T(1024)(128)(4,1)S(1)}, s32[]{:S(2)}) async-start(s8[8388608]{0:T(1024)(128)(4,1)} %bitcast.208), calls=%async_computation.9 | async-start | bytes 8388608
  270.9 2.7 slice-start.3
  372.5 7.3 copy-start
  379.8 113.0 %copy-start.4 = (f32[1,128,2048]{2,1,0:T(8,128)S(1)}, f32[1,128,2048]{2,1,0:T(8,128)}, u32[]{:S(2)}) copy-start(f32[1,128,2048]{2,1,0:T(8,128)} %param.10) | copy-start | bytes 3145732
  504.7 62.9 %all-to-all-start = ((bf16[7,128,2048]{1,0,2:T(8,128)(2,1)}), bf16[7,128,2048]{1,0,2:T(8,128)(2,1)}, u32[]{:S(2)}, u32[]{:S(2)}) async-start(bf16[7,128,2048]{1,0,2:T(8,128)(2,1)} %copy.72), calls=%async_computation | async-start | bytes 8388608 | tf_op jit(solution)/shard_map/all_to_all | solution.py:171
  661.3 26.4 %all-to-all-start.1 = ((bf16[8,2,16384]{2,1,0:T(2,128)(2,1)}), bf16[8,2,16384]{2,1,0:T(2,128)(2,1)}, u32[]{:S(2)}, u32[]{:S(2)}) async-start(bf16[8,2,16384]{2,1,0:T(2,128)(2,1)} %reshape.321), calls=%async_computation.1 | async-start | bytes 1048576 | tf_op jit(solution)/shard_map/all_to_all | solution.py:135
  687.7 35.4 %all-to-all-start.2 = ((bf16[3,1024,256]{2,0,1:T(4,128)(2,1)}), bf16[3,1024,256]{2,0,1:T(4,128)(2,1)}, u32[]{:S(2)}, u32[]{:S(2)}) async-start(bf16[3,1024,256]{2,0,1:T(4,128)(2,1)} %pad_maximum_fusion), calls=%async_computation.2 | async-start | bytes 4194304 | tf_op jit(solution)/shard_map/all_to_all | solution.py:135
  709.2 39.6 %collective-permute-start = (bf16[128,2048]{1,0:T(8,128)(2,1)}, bf16[128,2048]{1,0:T(8,128)(2,1)}, u32[]{:S(2)}, u32[]{:S(2)}) collective-permute-start(bf16[128,2048]{1,0:T(8,128)(2,1)} %fusion.58), channel_id=1, source_target_pairs={{0,8},{8,16},{16,24},{24,32},{32,40},{40,48},{48,56},{56,64},{64,7... | collective-permute-start | bytes 1572872 | tf_op jit(solution)/shard_map/ppermute | solution.py:12
  729.9 6.6 copy-start.6
  729.9 13.1 %slice-start = ((s8[8388608]{0:T(1024)(128)(4,1)}), s8[4194304]{0:T(1024)(128)(4,1)S(1)}, s32[]{:S(2)}) async-start(s8[8388608]{0:T(1024)(128)(4,1)} %bitcast.204), calls=%async_computation.7 | async-start | bytes 8388608
  730.0 13.1 %copy-start.5 = (bf16[1,128,8,256]{1,3,2,0:T(8,128)(2,1)S(1)}, bf16[1,128,8,256]{1,3,2,0:T(8,128)(2,1)}, u32[]{:S(2)}) copy-start(bf16[1,128,8,256]{1,3,2,0:T(8,128)(2,1)} %copy.92) | copy-start | bytes 1572868
  736.6 6.5 slice-start.1
  746.4 10.5 %collective-permute-start.1 = (bf16[128,2048]{1,0:T(8,128)(2,1)S(1)}, bf16[128,2048]{1,0:T(8,128)(2,1)S(1)}, u32[]{:S(2)}, u32[]{:S(2)}) collective-permute-start(bf16[128,2048]{1,0:T(8,128)(2,1)S(1)} %fusion.89), channel_id=1, source_target_pairs={{0,120},{8,0},{16,8},{24,16},{32,24},{40,32},{48,40},{56,48},{64,5... | collective-permute-start | bytes 1572872 | tf_op jit(solution)/shard_map/ppermute | solution.py:12
Sparse Core Ops, SparseCore 0:
  10.2 121.2 all-gather.10
  133.6 118.2 all-gather.8
  254.1 118.3 all-gather.12
  374.5 118.2 all-gather.14
where the time goes:
time: 777 us; the launch traced here: 765 us
  waiting for transfers between devices  492 us (63%)
  matrix products  112 us (14%)
  local copies, waits for them, and re-layouts  95 us (12%)
  other arithmetic  29.8 us (4%)
  starting transfers between devices  22.1 us (3%)
  between operations  14.4 us (2%)
    all_gather x1, waiting for transfers between devices, shards(): lax.all_gather(w_key[0], 'seq', axis=1, tiled=True)  118 us
    all_gather x1, waiting for transfers between devices, shards(): lax.all_gather(w_out[0], 'seq', axis=1, tiled=True)  110 us
    all_gather x1, waiting for transfers between devices, shards(): lax.all_gather(w_query[0], 'seq', axis=1, tiled=True)  108 us
    all_gather x1, waiting for transfers between devices, shards(): lax.all_gather(w_value[0], 'seq', axis=1, tiled=True)  80 us
    all_to_all x1, waiting for transfers between devices, shards(): lax.all_to_all(pieces, 'seq', split_axis=2, concat_axis=1, tiled=True)  56.6 us
    dot_general x4, matrix products, times_t(): lax.dot_general(left, right, (((1,), (1,)), ((), ())), preferred_element_...  23.4 us
  transfers between devices with their start and end apart: 9, of which 7 were waited for; matrix products, arithmetic and copies ran while one was open for 17% of the time, Pallas kernels for 0%

commit v1 on v0

--- a/solution.py
+++ b/solution.py
@@ -168,7 +168,10 @@
 
     attn_grad = jnp.dot(grad_low, all_out, preferred_element_type=jnp.float32).astype(jnp.bfloat16)
     pieces = jnp.stack(project_local(normed_fwd) + project_local(normed_bwd) + [attn_grad])
-    head_view = lax.all_to_all(pieces, "seq", split_axis=2, concat_axis=1, tiled=True)
+    head_view = jnp.concatenate(
+        lax.all_to_all(jnp.stack(jnp.split(pieces, lax.axis_size("seq"), axis=2)), "seq", 0, 0),
+        axis=1,
+    )
     attn = attend(head_view[0], head_view[1], head_view[2])
     attn_tokens = to_tokens(attn[None])[0]
     branch = times_t(attn_tokens, all_out)

time: 777 us -> 780 us (level)
  local copies, waits for them, and re-layouts: 95 us -> 106 us
    unnamed x32 -> x39, local copies, waits for them, and re-layouts: 14 us -> 26.7 us
where the time goes in v1:
time: 780 us; the launch traced here: 768 us
  waiting for transfers between devices  485 us (62%)
  matrix products  112 us (14%)
  local copies, waits for them, and re-layouts  106 us (14%)
  other arithmetic  29.8 us (4%)
  starting transfers between devices  21.8 us (3%)
  between operations  14.2 us (2%)
    all_gather x1, waiting for transfers between devices, shards(): lax.all_gather(w_key[0], 'seq', axis=1, tiled=True)  118 us
    all_gather x1, waiting for transfers between devices, shards(): lax.all_gather(w_out[0], 'seq', axis=1, tiled=True)  111 us
    all_gather x1, waiting for transfers between devices, shards(): lax.all_gather(w_query[0], 'seq', axis=1, tiled=True)  108 us
    all_gather x1, waiting for transfers between devices, shards(): lax.all_gather(w_value[0], 'seq', axis=1, tiled=True)  80 us
    all_to_all x1, waiting for transfers between devices, shards(): lax.all_to_all(jnp.stack(jnp.split(pieces, lax.axis_size('seq'), axis=2))...  49.6 us
    unnamed x39, local copies, waits for them, and re-layouts  26.7 us
    dot_general x4, matrix products, times_t(): lax.dot_general(left, right, (((1,), (1,)), ((), ())), preferred_element_...  23.3 us
  transfers between devices with their start and end apart: 9, of which 7 were waited for; matrix products, arithmetic and copies ran while one was open for 17% of the time, Pallas kernels for 0%

profile of v1, /device:TPU:1, one launch (start us, length us, event | category | flops | bytes accessed | tf_op | source)
XLA Modules:
  0.0 768.0 jit_solution(2046299653418429706)
XLA Ops:
  13.0 118.5 %all-gather.11.cloned.1.call-done = bf16[1,2048,2048]{2,1,0:T(8,128)(2,1)} async-done(((bf16[1,2048,256]{2,1,0:T(8,128)(2,1)}), bf16[1,2048,2048]{2,1,0:T(8,128)(2,1)}) %all-gather.11.cloned.1.call-update) | async-done | bytes 8388624 | tf_op jit(solution)/shard_map/all_gather | solution.py:151
  131.5 12.4 %copy.79 = bf16[2048,2048]{1,0:T(8,128)(2,1)} copy(bf16[2048,2048]{0,1:T(8,128)(2,1)} %bitcast.235) | data formatting | bytes 16777216 | tf_op jit(solution)/shard_map/dot_general | solution.py:162
  143.8 108.1 %all-gather.9.cloned.1.call-done = bf16[1,2048,2048]{2,1,0:T(8,128)(2,1)} async-done(((bf16[1,2048,256]{2,1,0:T(8,128)(2,1)}), bf16[1,2048,2048]{2,1,0:T(8,128)(2,1)}) %all-gather.9.cloned.1.call-update) | async-done | bytes 8388624 | tf_op jit(solution)/shard_map/all_gather | solution.py:150
  251.9 12.4 %copy.78 = bf16[2048,2048]{1,0:T(8,128)(2,1)} copy(bf16[2048,2048]{0,1:T(8,128)(2,1)} %bitcast.236) | data formatting | bytes 16777216 | tf_op jit(solution)/shard_map/dot_general | solution.py:159
  264.3 6.5 fusion.134
  292.4 80.0 %all-gather.13.cloned.1.call-done = bf16[1,2048,2048]{2,1,0:T(8,128)(2,1)} async-done(((bf16[1,2048,256]{2,1,0:T(8,128)(2,1)}), bf16[1,2048,2048]{2,1,0:T(8,128)(2,1)}) %all-gather.13.cloned.1.call-update) | async-done | bytes 8388624 | tf_op jit(solution)/shard_map/all_gather | solution.py:152
  372.5 5.7 fusion.76
  382.2 110.6 %all-gather.15.cloned.1.call-done = bf16[1,2048,2048]{2,1,0:T(8,128)(2,1)} async-done(((bf16[1,2048,256]{2,1,0:T(8,128)(2,1)}), bf16[1,2048,2048]{2,1,0:T(8,128)(2,1)}) %all-gather.15.cloned.1.call-update) | async-done | bytes 8388624 | tf_op jit(solution)/shard_map/all_gather | solution.py:153
  492.8 5.5 fusion.64
  512.8 4.5 all-to-all-start
  519.1 49.6 %all-to-all-done = bf16[8,7,128,256]{3,2,1,0:T(8,128)(2,1)} async-done(((bf16[8,7,128,256]{3,2,1,0:T(8,128)(2,1)}), bf16[8,7,128,256]{3,2,1,0:T(8,128)(2,1)}, u32[]{:S(2)}, u32[]{:S(2)}) %all-to-all-start) | async-done | bytes 3670048 | tf_op jit(solution)/shard_map/all_to_all | solution.py:172
  568.7 3.9 fusion.143
  586.4 5.7 fusion.102
  592.1 7.2 fusion.154
  599.3 5.9 fusion.86
  605.2 14.8 %fusion.82 = f32[1024,2,128]{0,2,1:T(8,128)} fusion(bf16[1024,2,128]{0,2,1:T(8,128)(2,1)} %copy.96, f32[2,1024,1024]{1,2,0:T(8,128)} %fusion.102, f32[2,1024,1024]{1,2,0:T(8,128)} %get-tuple-element.78, f32[2,1024]{1,0:T(2,128)S(1)} %get-tuple-element.77), kind=kOutput, calls=%fused_computation.51 | convolution fusion | flops 551554048 | bytes 18358272 | tf_op jit(solution)/shard_map/while/body/eval_jaxpr/hqk,qhd->khd/dot_general | solution.py:118
  619.9 14.6 %fusion.79 = f32[1024,2,128]{0,2,1:T(8,128)} fusion(bf16[1024,2,128]{0,2,1:T(8,128)(2,1)} %copy.94, f32[2,1024,1024]{1,2,0:T(8,128)} %fusion.102, f32[2,1024,1024]{1,2,0:T(8,128)} %get-tuple-element.78, f32[2,1024]{1,0:T(2,128)S(1)} %get-tuple-element.77), kind=kOutput, calls=%fused_computation.50 | convolution fusion | flops 551554048 | bytes 18358272 | tf_op jit(solution)/shard_map/while/body/eval_jaxpr/hqk,khd->qhd/dot_general | solution.py:115
  640.5 7.5 fusion.145
  648.0 5.2 fusion.85
  653.2 3.6 copy.88
  657.3 5.6 reduce
  664.9 4.1 all-to-all-start.1
  672.6 3.6 copy.102
  676.2 3.6 copy.100
  685.2 6.0 pad_maximum_fusion
  691.1 6.5 all-to-all-start.2
  705.3 7.3 fusion.58
  712.6 4.0 collective-permute-start
  716.5 9.9 %all-to-all-done.2 = bf16[3,1024,256]{2,0,1:T(4,128)(2,1)} async-done(((bf16[3,1024,256]{2,0,1:T(4,128)(2,1)}), bf16[3,1024,256]{2,0,1:T(4,128)(2,1)}, u32[]{:S(2)}, u32[]{:S(2)}) %all-to-all-start.2) | async-done | bytes 1572896 | tf_op jit(solution)/shard_map/all_to_all | solution.py:135
  733.3 6.6 fusion.13
  739.9 6.5 fusion.37
  754.3 5.9 collective-permute-done.1
  (98 shorter events, 102.4 us)
Async XLA Ops:
  7.2 124.3 %all-gather.11.cloned.1.call-start = ((), (), s32[]{:S(2)}) async-start(), calls=%async_computation.4 | async-start | bytes 9437184 | tf_op jit(solution)/shard_map/all_gather | solution.py:151
  7.9 244.0 %all-gather.9.cloned.1.call-start = ((), (), s32[]{:S(2)}) async-start(), calls=%async_computation.3 | async-start | bytes 9437184 | tf_op jit(solution)/shard_map/all_gather | solution.py:150
  8.6 363.8 %all-gather.13.cloned.1.call-start = ((), (), s32[]{:S(2)}) async-start(), calls=%async_computation.5 | async-start | bytes 9437184 | tf_op jit(solution)/shard_map/all_gather | solution.py:152
  9.4 483.4 %all-gather.15.cloned.1.call-start = ((), (), s32[]{:S(2)}) async-start(), calls=%async_computation.6 | async-start | bytes 9437184 | tf_op jit(solution)/shard_map/all_gather | solution.py:153
  251.9 12.4 %copy-start.2 = (f32[1,128,2048]{2,1,0:T(8,128)S(1)}, f32[1,128,2048]{2,1,0:T(8,128)}, u32[]{:S(2)}) copy-start(f32[1,128,2048]{2,1,0:T(8,128)} %param.9) | copy-start | bytes 3145732
  251.9 12.4 %copy-start.7 = (f32[1,2048]{1,0:T(1,128)S(1)}, f32[1,2048]{1,0:T(1,128)}, u32[]{:S(2)}) copy-start(f32[1,2048]{1,0:T(1,128)} %param.11) | copy-start | bytes 24580
  264.3 6.5 copy-start.1
  264.3 6.6 copy-start.3
  264.3 9.1 %slice-start.2 = ((s8[8388608]{0:T(1024)(128)(4,1)}), s8[4194304]{0:T(1024)(128)(4,1)S(1)}, s32[]{:S(2)}) async-start(s8[8388608]{0:T(1024)(128)(4,1)} %bitcast.231), calls=%async_computation.9 | async-start | bytes 8388608
  270.9 2.7 slice-start.3
  372.5 7.3 copy-start
  379.8 113.0 %copy-start.4 = (f32[1,128,2048]{2,1,0:T(8,128)S(1)}, f32[1,128,2048]{2,1,0:T(8,128)}, u32[]{:S(2)}) copy-start(f32[1,128,2048]{2,1,0:T(8,128)} %param.10) | copy-start | bytes 3145732
  512.8 55.9 %all-to-all-start = ((bf16[8,7,128,256]{3,2,1,0:T(8,128)(2,1)}), bf16[8,7,128,256]{3,2,1,0:T(8,128)(2,1)}, u32[]{:S(2)}, u32[]{:S(2)}) async-start(bf16[8,7,128,256]{3,2,1,0:T(8,128)(2,1)} %fusion.120), calls=%async_computation | async-start | bytes 7340032 | tf_op jit(solution)/shard_map/all_to_all | solution.py:172
  664.9 26.2 %all-to-all-start.1 = ((bf16[8,2,16384]{2,1,0:T(2,128)(2,1)}), bf16[8,2,16384]{2,1,0:T(2,128)(2,1)}, u32[]{:S(2)}, u32[]{:S(2)}) async-start(bf16[8,2,16384]{2,1,0:T(2,128)(2,1)} %reshape.326), calls=%async_computation.1 | async-start | bytes 1048576 | tf_op jit(solution)/shard_map/all_to_all | solution.py:135
  691.1 35.3 %all-to-all-start.2 = ((bf16[3,1024,256]{2,0,1:T(4,128)(2,1)}), bf16[3,1024,256]{2,0,1:T(4,128)(2,1)}, u32[]{:S(2)}, u32[]{:S(2)}) async-start(bf16[3,1024,256]{2,0,1:T(4,128)(2,1)} %pad_maximum_fusion), calls=%async_computation.2 | async-start | bytes 4194304 | tf_op jit(solution)/shard_map/all_to_all | solution.py:135
  712.6 39.7 %collective-permute-start = (bf16[128,2048]{1,0:T(8,128)(2,1)}, bf16[128,2048]{1,0:T(8,128)(2,1)}, u32[]{:S(2)}, u32[]{:S(2)}) collective-permute-start(bf16[128,2048]{1,0:T(8,128)(2,1)} %fusion.58), channel_id=1, source_target_pairs={{0,8},{8,16},{16,24},{24,32},{32,40},{40,48},{48,56},{56,64},{64,7... | collective-permute-start | bytes 1572872 | tf_op jit(solution)/shard_map/ppermute | solution.py:12
  733.3 6.6 copy-start.6
  733.3 13.1 %slice-start = ((s8[8388608]{0:T(1024)(128)(4,1)}), s8[4194304]{0:T(1024)(128)(4,1)S(1)}, s32[]{:S(2)}) async-start(s8[8388608]{0:T(1024)(128)(4,1)} %bitcast.227), calls=%async_computation.7 | async-start | bytes 8388608
  733.3 13.1 %copy-start.5 = (bf16[1,128,8,256]{1,3,2,0:T(8,128)(2,1)S(1)}, bf16[1,128,8,256]{1,3,2,0:T(8,128)(2,1)}, u32[]{:S(2)}) copy-start(bf16[1,128,8,256]{1,3,2,0:T(8,128)(2,1)} %copy.106) | copy-start | bytes 1572868
  739.9 6.5 slice-start.1
  749.8 10.5 %collective-permute-start.1 = (bf16[128,2048]{1,0:T(8,128)(2,1)S(1)}, bf16[128,2048]{1,0:T(8,128)(2,1)S(1)}, u32[]{:S(2)}, u32[]{:S(2)}) collective-permute-start(bf16[128,2048]{1,0:T(8,128)(2,1)S(1)} %fusion.89), channel_id=1, source_target_pairs={{0,120},{8,0},{16,8},{24,16},{32,24},{40,32},{48,40},{56,48},{64,5... | collective-permute-start | bytes 1572872 | tf_op jit(solution)/shard_map/ppermute | solution.py:12
Sparse Core Ops, SparseCore 0:
  10.2 121.2 all-gather.10
  133.6 118.2 all-gather.8
  254.1 118.3 all-gather.12
  374.5 118.2 all-gather.14
